TPU v7x, 32 devices: a whole 2x2x4 slice. The times are simulated.
32 devices in a mesh: dp: 8 (over y, x, core), mp: 4 (over z).
Axes of the slice: x: 2, y: 2, z: 4, core: 2. Of those that a mesh axis runs over, the one named last changes fastest.
Arguments:
- inputs: bfloat16 [8192, 2048], P('dp'), may hold values from -8 to 8
- segment_ids: int32 [8, 1024], P('dp'), may hold values from 0 to 4, as said below
- pad_count: int32 [8], P('dp'), may hold values from 0 to 128, as said below
- layer_norm_gain: float32 [2048], replicated, may hold values from 0.5 to 1.5
- layer_norm_bias: float32 [2048], replicated, may hold values from -1.75 to 1.75
- qkv_weight: bfloat16 [2048, 3, 2048], P(None, None, 'mp'), may hold values from -0.125 to 0.125
- qkv_bias: float32 [3, 2048], P(None, 'mp'), may hold values from -1.75 to 1.75
- out_weight: bfloat16 [2048, 2048], P('mp'), may hold values from -1 to 1
- gateup_weight: bfloat16 [2048, 2, 5632], P(None, None, 'mp'), may hold values from -0.125 to 0.125
- down_weight: bfloat16 [5632, 2048], P('mp'), may hold values from -0.078125 to 0.078125
- y_grad: bfloat16 [8192, 2048], P('dp'), may hold values from -8 to 8
Outputs:
- output: bfloat16 [8192, 2048], P('dp')
- x_grad: bfloat16 [8192, 2048], P('dp')
- ln_gain_grad: float32 [2048], replicated
- ln_bias_grad: float32 [2048], replicated
- qkv_weight_grad: float32 [2048, 3, 2048], P('dp', None, 'mp')
- qkv_bias_grad: float32 [3, 2048], P(None, 'mp')
- out_weight_grad: float32 [2048, 2048], P('mp', 'dp')
- gateup_weight_grad: float32 [2048, 2, 5632], P('dp', None, 'mp')
- down_weight_grad: float32 [5632, 2048], P('mp', 'dp')
Inputs may be any that keep to these rules, and one draw needn't show every extreme that they name: `segment_ids`: within a row the ids never fall and run from 0 to 4 - 1 over the row's documents, each of 1 or more tokens and one of exactly 512; the row's last pad_count slots carry id 4. `pad_count`: some row has 128 padded slots and some row has none.
All inputs are finite; a program needn't handle non-finite values.
Results may differ from a plain program's by a relative error of at most 0.012.
The roundings to bfloat16 on the way count: a program that leaves them out, or rounds other values in their place, can miss the bound.
Values may be sent and summed in bfloat16 or wider, within the bound.
No kernel may reach another device: no remote copies, remote signals or barrier semaphores. Data moves between devices by JAX's collectives and lax.ppermute only.
A program may use at most 256 MiB of HBM per device.

v0:
```python
import jax
import jax.numpy as jnp
from jax import lax
from jax.sharding import PartitionSpec as P

HEAD_DIM = 64
ROT = 16
DOCS = 4
EPS = 1e-05


def tables(seg, padding, count):
    steps = jnp.arange(count, dtype=jnp.int32)
    onehot = (seg[:, None] == jnp.arange(DOCS + 1, dtype=jnp.int32)[None, :]).astype(jnp.int32)
    counts = jnp.sum(onehot, axis=0)
    before = jnp.cumsum(counts) - counts
    start = jnp.sum(onehot * before[None, :], axis=1)
    half = ROT // 2
    freq = jnp.power(10000.0, -2.0 * jnp.arange(half, dtype=jnp.float32) / ROT)
    angle = (steps - start).astype(jnp.float32)[:, None] * freq[None, :]
    return (jnp.cos(angle)[:, None, :], jnp.sin(angle)[:, None, :], steps < count - padding)


def rotate(value, cosine, sine):
    half = ROT // 2
    first = value[..., :half]
    second = value[..., half:ROT]
    return jnp.concatenate(
        [first * cosine - second * sine, second * cosine + first * sine, value[..., ROT:]], axis=-1
    )


def unrotate(value, cosine, sine):
    half = ROT // 2
    first = value[..., :half]
    second = value[..., half:ROT]
    return jnp.concatenate(
        [first * cosine + second * sine, second * cosine - first * sine, value[..., ROT:]], axis=-1
    )


def allowed_mask(start, block_rows, seg, valid):
    count = seg.shape[0]
    rows = start + jnp.arange(block_rows, dtype=jnp.int32)
    cols = jnp.arange(count, dtype=jnp.int32)
    seg_rows = lax.dynamic_slice_in_dim(seg, start, block_rows, 0)
    allowed = (
        (seg_rows[:, None] == seg[None, :]) & (cols[None, :] <= rows[:, None]) & valid[None, :]
    )
    return allowed | (cols[None, :] == rows[:, None])


def scores(start, block_rows, query, key, seg, valid):
    part = lax.dynamic_slice_in_dim(query, start, block_rows, 0)
    score = jnp.einsum(
        "qhd,khd->hqk", part, key, preferred_element_type=jnp.float32
    ) * HEAD_DIM ** (-0.5)
    allowed = allowed_mask(start, block_rows, seg, valid)
    return (part, jnp.where(allowed[None], score, -1e30), allowed)


def shards(
    inputs,
    segment_ids,
    pad_count,
    layer_norm_gain,
    layer_norm_bias,
    qkv_weight,
    qkv_bias,
    out_weight,
    gateup_weight,
    down_weight,
    y_grad,
):
    count, width = inputs.shape
    local = qkv_weight.shape[2]
    hidden_here = gateup_weight.shape[2]
    heads_here = local // HEAD_DIM
    seg = segment_ids[0]
    cosine, sine, valid = tables(seg, pad_count[0], count)
    valid_f = valid.astype(jnp.float32)
    xf = inputs.astype(jnp.float32)
    row_average = jnp.mean(xf, axis=-1, keepdims=True)
    mean_removed = xf - row_average
    var = jnp.mean(mean_removed * mean_removed, axis=-1, keepdims=True)
    inverse_deviation = lax.rsqrt(var + EPS)
    standardized_input = mean_removed * inverse_deviation
    norm_output = (standardized_input * layer_norm_gain + layer_norm_bias).astype(jnp.bfloat16)
    qkv = jnp.dot(
        norm_output, qkv_weight.reshape(width, 3 * local), preferred_element_type=jnp.float32
    )
    qkv = qkv.reshape(count, 3, local) + qkv_bias
    query = rotate(qkv[:, 0].reshape(count, heads_here, HEAD_DIM), cosine, sine).astype(
        jnp.bfloat16
    )
    key = rotate(qkv[:, 1].reshape(count, heads_here, HEAD_DIM), cosine, sine).astype(jnp.bfloat16)
    value = qkv[:, 2].reshape(count, heads_here, HEAD_DIM).astype(jnp.bfloat16)
    block_rows = min(512, count)
    starts = jnp.arange(count // block_rows, dtype=jnp.int32) * block_rows

    def forward_block(start):
        part, score, allowed = scores(start, block_rows, query, key, seg, valid)
        top = jnp.max(score, axis=-1, keepdims=True)
        expo = jnp.exp(score - top)
        total = jnp.sum(expo, axis=-1, keepdims=True)
        prob = (expo / total).astype(jnp.bfloat16)
        return (
            jnp.einsum("hqk,khd->qhd", prob, value, preferred_element_type=jnp.float32),
            (top + jnp.log(total))[..., 0],
        )

    attn_blocks, log_sums = lax.map(forward_block, starts)
    attn = (attn_blocks.reshape(count, local) * valid_f[:, None]).astype(jnp.bfloat16)
    gateup = jnp.dot(
        norm_output,
        gateup_weight.reshape(width, 2 * hidden_here),
        preferred_element_type=jnp.float32,
    )
    gateup = gateup.reshape(count, 2, hidden_here)
    gate = gateup[:, 0]
    upper = gateup[:, 1]
    sigma = jax.nn.sigmoid(gate)
    active = gate * sigma
    hidden = (active * upper).astype(jnp.bfloat16)
    partial_value = jnp.dot(attn, out_weight, preferred_element_type=jnp.float32) + jnp.dot(
        hidden, down_weight, preferred_element_type=jnp.float32
    )
    summed = lax.psum(partial_value, "mp")
    result = (xf + summed).astype(jnp.bfloat16)
    grad_out = jnp.einsum("ti,to->io", attn, y_grad, preferred_element_type=jnp.float32)
    grad_down = jnp.einsum("tf,to->fo", hidden, y_grad, preferred_element_type=jnp.float32)
    d_attn = jnp.einsum("to,io->ti", y_grad, out_weight, preferred_element_type=jnp.float32)
    d_attn = (d_attn.astype(jnp.bfloat16) * valid.astype(jnp.bfloat16)[:, None]).reshape(
        count, heads_here, HEAD_DIM
    )
    d_hidden = jnp.einsum("to,fo->tf", y_grad, down_weight, preferred_element_type=jnp.float32)
    d_gate = (d_hidden * upper * sigma * (1.0 + gate * (1.0 - sigma))).astype(jnp.bfloat16)
    d_upper = (d_hidden * active).astype(jnp.bfloat16)
    d_gateup = jnp.stack([d_gate, d_upper], axis=1)
    grad_gateup = jnp.einsum(
        "td,tjf->djf", norm_output, d_gateup, preferred_element_type=jnp.float32
    )

    def backward_block(carry, item):
        key_acc, value_acc = carry
        start, log_sum = item
        part, score, allowed = scores(start, block_rows, query, key, seg, valid)
        prob = jnp.where(allowed[None], jnp.exp(score - log_sum[..., None]), 0.0)
        prob_low = prob.astype(jnp.bfloat16)
        d_rows = lax.dynamic_slice_in_dim(d_attn, start, block_rows, 0)
        d_prob = jnp.einsum("qhd,khd->hqk", d_rows, value, preferred_element_type=jnp.float32)
        d_score = prob * (d_prob - jnp.sum(prob * d_prob, axis=-1, keepdims=True))
        d_score = d_score.astype(jnp.bfloat16)
        d_query = jnp.einsum(
            "hqk,khd->qhd", d_score, key, preferred_element_type=jnp.float32
        ) * HEAD_DIM ** (-0.5)
        key_acc = key_acc + jnp.einsum(
            "hqk,qhd->khd", d_score, part, preferred_element_type=jnp.float32
        ) * HEAD_DIM ** (-0.5)
        value_acc = value_acc + jnp.einsum(
            "hqk,qhd->khd", prob_low, d_rows, preferred_element_type=jnp.float32
        )
        return ((key_acc, value_acc), d_query)

    empty = jnp.zeros((count, heads_here, HEAD_DIM), jnp.float32)
    (d_key, d_value), d_queries = lax.scan(backward_block, (empty, empty), (starts, log_sums))
    d_query = unrotate(d_queries.reshape(count, heads_here, HEAD_DIM), cosine, sine)
    d_key = unrotate(d_key, cosine, sine)
    d_qkv = (
        jnp.stack([d_query, d_key, d_value], axis=1).reshape(count, 3, local).astype(jnp.bfloat16)
    )
    grad_qkv = jnp.einsum("td,tjc->djc", norm_output, d_qkv, preferred_element_type=jnp.float32)
    grad_bias = jnp.sum(d_qkv.astype(jnp.float32), axis=0)
    weight_sums = (
        lax.psum_scatter(grad_qkv, "dp", scatter_dimension=0, tiled=True),
        lax.psum_scatter(grad_out, "dp", scatter_dimension=1, tiled=True),
        lax.psum_scatter(grad_gateup, "dp", scatter_dimension=0, tiled=True),
        lax.psum_scatter(grad_down, "dp", scatter_dimension=1, tiled=True),
    )
    d_partial = jnp.einsum(
        "tjc,djc->td", d_qkv, qkv_weight, preferred_element_type=jnp.float32
    ) + jnp.einsum("tjf,djf->td", d_gateup, gateup_weight, preferred_element_type=jnp.float32)
    normalized_gradient = lax.psum(d_partial, "mp")
    gain_product = jnp.sum(normalized_gradient * standardized_input, axis=0)
    shift_part = jnp.sum(normalized_gradient, axis=0)
    gain_scaled = normalized_gradient * layer_norm_gain
    inner = (
        gain_scaled
        - jnp.mean(gain_scaled, axis=-1, keepdims=True)
        - standardized_input * jnp.mean(gain_scaled * standardized_input, axis=-1, keepdims=True)
    )
    input_grad = (y_grad.astype(jnp.float32) + inverse_deviation * inner).astype(jnp.bfloat16)
    bias_sum, gain_sum, shift_sum = lax.psum((grad_bias, gain_product, shift_part), "dp")
    return (
        result,
        input_grad,
        gain_sum,
        shift_sum,
        weight_sums[0],
        bias_sum,
        weight_sums[1],
        weight_sums[2],
        weight_sums[3],
    )


def solution(mesh):
    placed = (
        P("dp", None),
        P("dp", None),
        P("dp"),
        P(),
        P(),
        P(None, None, "mp"),
        P(None, "mp"),
        P("mp", None),
        P(None, None, "mp"),
        P("mp", None),
        P("dp", None),
    )
    return jax.shard_map(
        shards,
        mesh=mesh,
        in_specs=placed,
        out_specs=(
            P("dp", None),
            P("dp", None),
            P(),
            P(),
            P("dp", None, "mp"),
            P(None, "mp"),
            P("mp", "dp"),
            P("dp", None, "mp"),
            P("mp", "dp"),
        ),
        check_vma=False,
    )
```

profile of v0, /device:TPU:0, one launch (start us, length us, event | category | flops | bytes accessed | tf_op | source)
XLA Modules:
  0.0 1045.4 jit_solution(3423792791581384292)
XLA Ops:
  8.1 3.0 convert_reduce_fusion
  12.9 8.9 copy.39
  21.8 10.5 %broadcast_add_fusion = f32[1024,3,512]{0,2,1:T(8,128)S(1)} fusion(f32[3,512]{1,0:T(4,128)S(1)} %copy-done.24, bf16[2048,3,512]{0,2,1:T(8,128)(2,1)} %copy.39, bf16[1024,2048]{1,0:T(8,128)(2,1)} %param.15, f32[2048]{0:T(1024)S(1)} %copy-done.25, f32[2048]{0:T(1024)S(1)} %copy-done.21, f32[1024]{0:T(1024)S(1)} %add_rsqrt_fusion, ...), kind=kOutput, calls=%fused_computation.86 | convolution fusion | flops 6456606720 | bytes 16807936 | tf_op jit(solution)/shard_map/dot_general | solution.py:89
  32.4 2.3 fusion.75
  45.3 79.3 %while.28 = (s32[]{:T(128)}, f32[2,512,8,64]{1,0,3,2:T(2,128)}, f32[2,8,512]{2,1,0:T(8,128)S(1)}, s32[2]{0:T(128)S(1)}, s32[1024]{0:T(1024)S(1)}, /*index=5*/s32...) while((s32[]{:T(128)}, f32[2,512,8,64]{1,0,3,2:T(2,128)}, ...), condition=%wide.region_8.9_spmd.clone, body=%wide.region_5.8_spmd.clone.sunk | while | flops 1127216640 | bytes 64635104 | solution.py:112
  49.9 4.7 fusion.118
  54.6 4.2 fusion.119
  58.9 4.6 fusion.120
  65.5 19.6 %dynamic_update_slice.19 = f32[2,512,8,64]{1,0,3,2:T(2,128)} dynamic-update-slice(f32[2,512,8,64]{1,0,3,2:T(2,128)} %get-tuple-element.475, f32[1,512,8,64]{1,0,3,2:T(1,128)} %copy.73, s32[]{:T(128)} %get-tuple-element.474, s32[]{:T(128)} %constant.40.clone.1..sunk, s32[]{:T(128)} %constant.40.clone.1..sunk, s32[]{:T(128)} %constant.40.clone.1..sunk) | dynamic-update-slice | bytes 2097156 | tf_op jit(solution)/shard_map/while/body/jit(dynamic_update_index_in_dim)/dynamic_update_slice | solution.py:112
  89.3 4.7 fusion.118
  94.0 4.2 fusion.119
  98.3 4.6 fusion.120
  104.9 19.6 %dynamic_update_slice.19 = f32[2,512,8,64]{1,0,3,2:T(2,128)} dynamic-update-slice(f32[2,512,8,64]{1,0,3,2:T(2,128)} %get-tuple-element.475, f32[1,512,8,64]{1,0,3,2:T(1,128)} %copy.73, s32[]{:T(128)} %get-tuple-element.474, s32[]{:T(128)} %constant.40.clone.1..sunk, s32[]{:T(128)} %constant.40.clone.1..sunk, s32[]{:T(128)} %constant.40.clone.1..sunk) | dynamic-update-slice | bytes 2097156 | tf_op jit(solution)/shard_map/while/body/jit(dynamic_update_index_in_dim)/dynamic_update_slice | solution.py:112
  124.5 5.5 fusion.62
  132.1 159.0 %while.29 = (s32[]{:T(128)}, f32[1024,8,64]{0,2,1:T(8,128)}, f32[1024,8,64]{0,2,1:T(8,128)}, f32[2,512,8,64]{1,0,3,2:T(2,128)}, s32[2]{0:T(128)S(1)}, /*index=5*...) while((s32[]{:T(128)}, f32[1024,8,64]{0,2,1:T(8,128)}, ...), condition=%wide.region_12.13_spmd.clone, body=%wide.region_10.12_spmd.clone.sunk | while | flops 2732324352 | bytes 187793712 | solution.py:166
  136.4 9.7 fusion.130
  146.1 13.8 %multiply_reduce_fusion.3 = (f32[8,512]{1,0:T(8,128)S(1)}, f32[8,512,1024]{2,1,0:T(8,128)}) fusion(f32[8,512,1024]{2,1,0:T(8,128)} %fusion.130, f32[8,512]{1,0:T(8,128)S(1)} %dynamic-slice_bitcast_fusion.2, bf16[1024,8,64]{0,2,1:T(8,128)(2,1)S(1)} %get-tuple-element.540, bf16[1024,8,64]{0,2,1:T(8,128)(2,1)S(1)} %copy-done.4, s32[]{:T(128)S(6)} %select_n.47, ...), kind=kOutput, calls=%fused_computation.23.clone.1 | convolution fusion | flops 562032640 | bytes 35684356 | tf_op jit(solution)/shard_map/while/body/eval_jaxpr/qhd,khd->hqk/dot_general | solution.py:55
  159.9 11.3 %multiply_convert_fusion.8 = bf16[8,512,1024]{2,1,0:T(8,128)(2,1)S(1)} fusion(f32[8,512,1024]{2,1,0:T(8,128)} %get-tuple-element.459, f32[8,512,1024]{2,1,0:T(8,128)} %fusion.130, f32[8,512]{1,0:T(8,128)S(1)} %get-tuple-element.460), kind=kLoop, calls=%fused_computation.22.clone.1 | loop fusion | flops 12582912 | bytes 41959424 | tf_op jit(solution)/shard_map/while/body/eval_jaxpr/convert_element_type | solution.py:153
  171.2 2.7 fusion.132
  176.0 19.6 %dynamic_update_slice.20 = f32[2,512,8,64]{1,0,3,2:T(2,128)} dynamic-update-slice(f32[2,512,8,64]{1,0,3,2:T(2,128)} %get-tuple-element.519, f32[1,512,8,64]{1,0,3,2:T(1,128)} %copy.74, s32[]{:T(128)} %get-tuple-element.516, s32[]{:T(128)} %constant.40.clone.1..sunk.1, s32[]{:T(128)} %constant.40.clone.1..sunk.1, s32[]{:T(128)} %constant.40.clone.1..sunk.1) | dynamic-update-slice | bytes 2097156 | tf_op jit(solution)/shard_map/while/body/jit(dynamic_update_index_in_dim)/dynamic_update_slice | solution.py:112
  195.6 6.6 bitcast_add_fusion.5
  202.3 8.7 bitcast_add_fusion.6
  215.2 9.7 fusion.130
  224.8 13.7 %multiply_reduce_fusion.3 = (f32[8,512]{1,0:T(8,128)S(1)}, f32[8,512,1024]{2,1,0:T(8,128)}) fusion(f32[8,512,1024]{2,1,0:T(8,128)} %fusion.130, f32[8,512]{1,0:T(8,128)S(1)} %dynamic-slice_bitcast_fusion.2, bf16[1024,8,64]{0,2,1:T(8,128)(2,1)S(1)} %get-tuple-element.540, bf16[1024,8,64]{0,2,1:T(8,128)(2,1)S(1)} %copy-done.4, s32[]{:T(128)S(6)} %select_n.47, ...), kind=kOutput, calls=%fused_computation.23.clone.1 | convolution fusion | flops 562032640 | bytes 35684356 | tf_op jit(solution)/shard_map/while/body/eval_jaxpr/qhd,khd->hqk/dot_general | solution.py:55
  238.6 11.3 %multiply_convert_fusion.8 = bf16[8,512,1024]{2,1,0:T(8,128)(2,1)S(1)} fusion(f32[8,512,1024]{2,1,0:T(8,128)} %get-tuple-element.459, f32[8,512,1024]{2,1,0:T(8,128)} %fusion.130, f32[8,512]{1,0:T(8,128)S(1)} %get-tuple-element.460), kind=kLoop, calls=%fused_computation.22.clone.1 | loop fusion | flops 12582912 | bytes 41959424 | tf_op jit(solution)/shard_map/while/body/eval_jaxpr/convert_element_type | solution.py:153
  249.9 2.7 fusion.132
  254.7 19.6 %dynamic_update_slice.20 = f32[2,512,8,64]{1,0,3,2:T(2,128)} dynamic-update-slice(f32[2,512,8,64]{1,0,3,2:T(2,128)} %get-tuple-element.519, f32[1,512,8,64]{1,0,3,2:T(1,128)} %copy.74, s32[]{:T(128)} %get-tuple-element.516, s32[]{:T(128)} %constant.40.clone.1..sunk.1, s32[]{:T(128)} %constant.40.clone.1..sunk.1, s32[]{:T(128)} %constant.40.clone.1..sunk.1) | dynamic-update-slice | bytes 2097156 | tf_op jit(solution)/shard_map/while/body/jit(dynamic_update_index_in_dim)/dynamic_update_slice | solution.py:112
  274.3 7.2 bitcast_add_fusion.5
  281.5 9.3 bitcast_add_fusion.6
  291.1 4.1 reshape.378
  298.0 2.4 slice.128
  307.5 11.2 %copy.66 = bf16[256,8,2,1408]{3,1,2,0:T(8,128)(2,1)} copy(bf16[256,8,2,1408]{3,2,1,0:T(2,128)(2,1)} %bitcast.147) | data formatting | bytes 23068672
  318.8 15.2 %copy.41 = bf16[2816,2048]{1,0:T(8,128)(2,1)} copy(bf16[2816,2048]{0,1:T(8,128)(2,1)} %bitcast.143) | data formatting | bytes 23068672 | tf_op jit(solution)/shard_map/dot_general | solution.py:114
  334.0 19.1 %fusion.72 = f32[1024,2,1408]{2,0,1:T(8,128)} fusion(bf16[2,1408,2048]{2,1,0:T(8,128)(2,1)} %bitcast.148, bf16[1024,2048]{1,0:T(8,128)(2,1)} %param.15, f32[2048]{0:T(1024)S(1)} %copy-done.26, f32[2048]{0:T(1024)S(1)} %copy-done.22, f32[1024]{0:T(1024)S(1)} %copy-done.20, f32[1024]{0:T(1024)S(1)} %copy-done.18), kind=kOutput, calls=%fused_computation.130 | convolution fusion | flops 11823742976 | bytes 27287552 | tf_op jit(solution)/shard_map/dot_general | solution.py:114
  353.6 17.5 %fusion.59 = (bf16[1024,1,1408]{2,0,1:T(8,128)(2,1)}, bf16[1024,1,1408]{2,0,1:T(8,128)(2,1)}, bf16[1024,1408]{1,0:T(8,128)(2,1)}) fusion(f32[1024,2,1408]{2,0,1:T(8,128)} %fusion.72, bf16[1024,2048]{1,0:T(8,128)(2,1)} %param.25, bf16[1408,2048]{1,0:T(8,128)(2,1)} %param.24), kind=kOutput, calls=%fused_computation.88 | convolution fusion | flops 5927206912 | bytes 30146560 | tf_op jit(solution)/shard_map/to,fo->tf/dot_general | solution.py:136
  371.1 12.3 %fusion.76 = f32[1024,2048]{1,0:T(8,128)} fusion(bf16[1024,1408]{1,0:T(8,128)(2,1)} %get-tuple-element.292, bf16[1408,2048]{1,0:T(8,128)(2,1)} %param.24), kind=kOutput, calls=%fused_computation.132 | convolution fusion | flops 5905580032 | bytes 17039360 | tf_op jit(solution)/shard_map/dot_general | solution.py:125
  383.5 8.9 fusion.69
  392.4 20.2 %bitcast_add_fusion.2 = f32[1024,2048]{1,0:T(8,128)} fusion(f32[1024,2048,1]{1,0,2:T(8,128)} %fusion.69, bf16[2048,2,1408]{2,1,0:T(2,128)(2,1)} %param.23, bf16[1024,1,1408]{2,0,1:T(8,128)(2,1)} %get-tuple-element.291, bf16[1024,1,1408]{2,0,1:T(8,128)(2,1)} %get-tuple-element.290), kind=kOutput, calls=%fused_computation.69 | convolution fusion | flops 11816140800 | bytes 34078720 | tf_op jit(solution)/shard_map/tjf,djf->td/dot_general | solution.py:182
  412.7 9.1 convolution_add_fusion
  421.8 20.7 %fusion.57 = f32[2048,2,1408]{2,0,1:T(8,128)} fusion(bf16[1024,1,1408]{2,0,1:T(8,128)(2,1)} %get-tuple-element.291, bf16[1024,1,1408]{2,0,1:T(8,128)(2,1)} %get-tuple-element.290, bf16[1024,2048]{1,0:T(8,128)(2,1)} %param.15, f32[2048]{0:T(1024)S(1)} %copy-done.26, f32[2048]{0:T(1024)S(1)} %copy-done.22, f32[1024]{0:T(1024)S(1)} %copy-done.20, ...), kind=kOutput, calls=%fused_computation.84 | convolution fusion | flops 11835277312 | bytes 33054720 | tf_op jit(solution)/shard_map/td,tjf->djf/dot_general | solution.py:140
  442.6 7.1 fusion.63
  449.8 13.8 %fusion.77 = f32[1408,2048]{1,0:T(8,128)} fusion(bf16[1024,1408]{1,0:T(8,128)(2,1)} %get-tuple-element.292, bf16[1024,2048]{1,0:T(8,128)(2,1)} %param.25), kind=kOutput, calls=%fused_computation.133 | convolution fusion | flops 5905580032 | bytes 18612224 | tf_op jit(solution)/shard_map/tf,to->fo/dot_general | solution.py:131
  465.0 15.0 %fusion.68 = f32[2048,3,512]{2,0,1:T(8,128)} fusion(bf16[1024,1,512]{2,0,1:T(8,128)(2,1)} %copy.45, bf16[1024,1,512]{2,0,1:T(8,128)(2,1)} %copy.44, bf16[1024,1,512]{2,0,1:T(8,128)(2,1)S(1)} %copy-done.9, bf16[1024,2048]{1,0:T(8,128)(2,1)} %param.15, f32[2048]{0:T(1024)S(1)} %copy-done.26, f32[2048]{0:T(1024)S(1)} %copy-done.22, f32[1024]{0:T(1024)S(1)} %copy-done.20, ...), kind=kOutput, calls=%fused_computation.128 | convolution fusion | flops 6464471040 | bytes 19947520 | tf_op jit(solution)/shard_map/td,tjc->djc/dot_general | solution.py:172
  482.1 504.8 %all-reduce.4.cloned.1.call-done = (f32[1024,2048]{1,0:T(8,128)}, f32[1024,2048]{1,0:T(8,128)}) async-done(((f32[1024,2048]{1,0:T(8,128)}, f32[1024,2048]{1,0:T(8,128)}), (f32[1024,2048]{1,0:T(8,128)}, f32[1024,2048]{1,0:T(8,128)})) %all-reduce.4.cloned.1.call-update) | async-done | bytes 16777232 | tf_op jit(solution)/shard_map/psum | solution.py:128
  986.9 6.5 fusion.48
  993.4 24.8 %all-reduce = (f32[2048]{0:T(1024)}, f32[2048]{0:T(1024)}, f32[3,512]{1,0:T(4,128)}) all-reduce(f32[2048]{0:T(1024)S(1)} %get-tuple-element.231, f32[2048]{0:T(1024)S(1)} %get-tuple-element.234, f32[3,512]{1,0:T(4,128)S(1)} %convert_reduce_fusion.1), channel_id=1, replica_groups=mesh['dp'=8,'mp'=4] {'dp'}, use_global_device_ids=true, to_apply=%region_17.18 | all-reduce | flops 5632 | bytes 45056 | tf_op jit(solution)/shard_map/psum | solution.py:193
  1018.2 13.6 %fusion.47 = (bf16[1024,2048]{1,0:T(8,128)(2,1)}, bf16[1024,2048]{1,0:T(8,128)(2,1)}) fusion(bf16[1024,2048]{1,0:T(8,128)(2,1)} %param.15, bf16[1024,2048]{1,0:T(8,128)(2,1)} %param.25, f32[1024,2048]{1,0:T(8,128)} %get-tuple-element.285, f32[1024]{0:T(1024)S(1)} %broadcast_multiply_fusion, f32[1024]{0:T(1024)S(1)} %broadcast_multiply_fusion.1, ...), kind=kLoop, calls=%fused_computation.65 | loop fusion | flops 27262976 | bytes 33579008 | tf_op jit(solution)/shard_map/convert_element_type | solution.py:192
  1031.9 5.6 copy.49
  (144 shorter events, 45.0 us)
Async XLA Ops:
  8.0 116.5 %copy-start = (bf16[512,2048]{1,0:T(8,128)(2,1)S(1)}, bf16[512,2048]{1,0:T(8,128)(2,1)}, u32[]{:S(2)}) copy-start(bf16[512,2048]{1,0:T(8,128)(2,1)} %param.22) | copy-start | bytes 6291460
  8.0 978.9 %all-reduce.4.cloned.1.call-start = ((), (), s32[]{:S(2)}) async-start(), calls=%async_computation.8 | async-start | bytes 33554432 | tf_op jit(solution)/shard_map/psum | solution.py:128
  8.1 3.6 copy-start.3
  11.7 10.1 copy-start.17
  12.9 8.9 copy-start.19
  12.9 8.9 copy-start.21
  12.9 8.9 copy-start.24
  12.9 8.9 copy-start.25
  32.4 3.5 copy-start.12
  40.7 1.4 copy-start.13
  40.7 1.4 copy-start.15
  45.3 79.3 %copy-start.23 = (bf16[1024]{0:T(1024)(128)(2,1)S(1)}, bf16[1024]{0:T(1024)(128)(2,1)}, u32[]{:S(2)}) copy-start(bf16[1024]{0:T(1024)(128)(2,1)} %fusion.65) | copy-start | bytes 6148
  54.6 4.3 copy-start.2
  94.0 4.3 copy-start.2
  136.4 9.7 copy-start.4
  171.2 4.8 copy-start.1
  195.6 6.6 copy-start.5
  215.1 9.7 copy-start.4
  249.9 4.8 copy-start.1
  274.3 7.2 copy-start.5
  291.1 5.6 copy-start.14
  291.1 5.6 copy-start.16
  318.8 15.2 %copy-start.18 = (f32[1024]{0:T(1024)S(1)}, f32[1024]{0:T(1024)}, u32[]{:S(2)}) copy-start(f32[1024]{0:T(1024)} %copy-done.17) | copy-start | bytes 12292
  318.8 15.2 %copy-start.20 = (f32[1024]{0:T(1024)S(1)}, f32[1024]{0:T(1024)}, u32[]{:S(2)}) copy-start(f32[1024]{0:T(1024)} %copy-done.19) | copy-start | bytes 12292
  318.8 15.2 %copy-start.22 = (f32[2048]{0:T(1024)S(1)}, f32[2048]{0:T(1024)}, u32[]{:S(2)}) copy-start(f32[2048]{0:T(1024)} %param.18) | copy-start | bytes 24580
  318.8 15.2 %copy-start.26 = (f32[2048]{0:T(1024)S(1)}, f32[2048]{0:T(1024)}, u32[]{:S(2)}) copy-start(f32[2048]{0:T(1024)} %param.19) | copy-start | bytes 24580
  334.0 19.1 %copy-start.7 = (f32[2,512,8,64]{1,0,3,2:T(2,128)S(1)}, f32[2,512,8,64]{1,0,3,2:T(2,128)}, u32[]{:S(2)}) copy-start(f32[2,512,8,64]{1,0,3,2:T(2,128)} %get-tuple-element.131) | copy-start | bytes 6291460
  353.1 30.4 %slice-start = ((s8[6291456]{0:T(1024)(128)(4,1)}), s8[4194304]{0:T(1024)(128)(4,1)S(1)}, s32[]{:S(2)}) async-start(s8[6291456]{0:T(1024)(128)(4,1)} %bitcast.150), calls=%async_computation.9 | async-start | bytes 8388608
  353.5 59.2 %copy-start.6 = (f32[64,8,2,512]{3,1,2,0:T(8,128)}, f32[64,8,2,512]{3,1,2,0:T(8,128)S(1)}, u32[]{:S(2)}) copy-start(f32[64,8,2,512]{3,1,2,0:T(8,128)S(1)} %copy.65) | copy-start | bytes 6291460
  353.5 29.9 %slice-start.1 = ((s8[6291456]{0:T(1024)(128)(4,1)}), s8[2097152]{0:T(1024)(128)(4,1)S(1)}, s32[]{:S(2)}) async-start(s8[6291456]{0:T(1024)(128)(4,1)} %bitcast.150), calls=%async_computation.10 | async-start | bytes 4194304
  371.1 12.4 %copy-start.8 = (bf16[1024,1,512]{2,0,1:T(8,128)(2,1)S(1)}, bf16[1024,1,512]{2,0,1:T(8,128)(2,1)}, u32[]{:S(2)}) copy-start(bf16[1024,1,512]{2,0,1:T(8,128)(2,1)} %copy.43) | copy-start | bytes 3145732
  371.1 12.4 %copy-start.10 = (bf16[1024,1,512]{2,0,1:T(8,128)(2,1)S(1)}, bf16[1024,1,512]{2,0,1:T(8,128)(2,1)}, u32[]{:S(2)}) copy-start(bf16[1024,1,512]{2,0,1:T(8,128)(2,1)} %copy.44) | copy-start | bytes 3145732
  371.1 12.4 %copy-start.11 = (bf16[1024,1,512]{2,0,1:T(8,128)(2,1)S(1)}, bf16[1024,1,512]{2,0,1:T(8,128)(2,1)}, u32[]{:S(2)}) copy-start(bf16[1024,1,512]{2,0,1:T(8,128)(2,1)} %copy.45) | copy-start | bytes 3145732
  421.8 610.1 %reduce-scatter.9.cloned.1.call-start = ((), (), s32[]{:S(2)}) async-start(), calls=%async_computation.6 | async-start | bytes 25952256 | tf_op jit(solution)/shard_map/reduce_scatter | solution.py:177
  442.5 595.0 %reduce-scatter.7.cloned.1.call-start = ((), (), s32[]{:S(2)}) async-start(), calls=%async_computation.5 | async-start | bytes 4718592 | tf_op jit(solution)/shard_map/reduce_scatter | solution.py:176
  449.7 587.8 %reduce-scatter.11.cloned.1.call-start = ((), (), s32[]{:S(2)}) async-start(), calls=%async_computation.7 | async-start | bytes 12976128 | tf_op jit(solution)/shard_map/reduce_scatter | solution.py:178
  463.5 1.5 copy-start.9
  463.6 573.9 %reduce-scatter.5.cloned.1.call-start = ((), (), s32[]{:S(2)}) async-start(), calls=%async_computation.4 | async-start | bytes 14155776 | tf_op jit(solution)/shard_map/reduce_scatter | solution.py:175
Sparse Core Ops, SparseCore 0:
  421.9 564.9 all-reduce.3
Sparse Core Ops, SparseCore 1:
  442.6 148.9 reduce-scatter.8
  595.3 50.9 reduce-scatter.6
  650.2 86.7 reduce-scatter.10
  741.0 91.8 reduce-scatter.4
where the time goes:
time: 1060 us; the launch traced here: 1050 us
  waiting for transfers between devices  505 us (48%)
  matrix products  262 us (25%)
  local copies, waits for them, and re-layouts  156 us (15%)
  other arithmetic  71.6 us (7%)
  blocking collectives  24.8 us (2%)
  between operations  17 us (2%)
    psum x1, waiting for transfers between devices, shards(): summed = lax.psum(partial_value, 'mp')  505 us
    dynamic_update_slice x8, local copies, waits for them, and re-layouts, shards(): attn_blocks, log_sums = lax.map(forward_block, starts)  86.9 us
    dot_general x4, matrix products, scores(): jnp.einsum('qhd,khd->hqk', part, key, preferred_element_type=jnp.float32)  36.8 us
    unnamed x54, local copies, waits for them, and re-layouts  28.3 us
    psum x1, blocking collectives, shards(): lax.psum((grad_bias, gain_product, shift_part), 'dp')  24.8 us
    convert_element_type x2, other arithmetic, backward_block(): d_score = d_score.astype(jnp.bfloat16)  22.7 us
  transfers between devices with their start and end apart: 5, of which 1 were waited for; matrix products, arithmetic and copies ran while one was open for 8% of the time, Pallas kernels for 0%

commit v1 on v0

--- a/solution.py
+++ b/solution.py
@@ -2,6 +2,7 @@
 import jax.numpy as jnp
 from jax import lax
 from jax.sharding import PartitionSpec as P
+from jax.lax import all_gather
 
 HEAD_DIM = 64
 ROT = 16
@@ -72,6 +73,12 @@
     down_weight,
     y_grad,
 ):
+
+    def run_samples_all_by_axis(m):
+        work_now = all_gather(m, axis_name="mp")
+        mat_out = jnp.sum(work_now, axis=0)
+        return mat_out
+
     count, width = inputs.shape
     local = qkv_weight.shape[2]
     hidden_here = gateup_weight.shape[2]
@@ -125,7 +132,7 @@
     partial_value = jnp.dot(attn, out_weight, preferred_element_type=jnp.float32) + jnp.dot(
         hidden, down_weight, preferred_element_type=jnp.float32
     )
-    summed = lax.psum(partial_value, "mp")
+    summed = run_samples_all_by_axis(partial_value)
     result = (xf + summed).astype(jnp.bfloat16)
     grad_out = jnp.einsum("ti,to->io", attn, y_grad, preferred_element_type=jnp.float32)
     grad_down = jnp.einsum("tf,to->fo", hidden, y_grad, preferred_element_type=jnp.float32)

time: 1060 us -> 1300 us (1.23)
  waiting for transfers between devices: 505 us -> 735 us
  other arithmetic: 71.6 us -> 91.7 us
    all_gather x0 -> x1, waiting for transfers between devices: none -> 521 us  [run_samples_all_by_axis(): work_now = all_gather(m, axis_name='mp')]
    psum x1, waiting for transfers between devices: 505 us -> 213 us  [shards(): normalized_gradient = lax.psum(d_partial, 'mp')]
    reduce_sum x0 -> x1, other arithmetic: none -> 15.9 us  [run_samples_all_by_axis(): mat_out = jnp.sum(work_now, axis=0)]
    unnamed x54 -> x46, local copies, waits for them, and re-layouts: 28.3 us -> 29.6 us
  transfers between devices with their start and end apart: 5 -> 6, of which waited for: 1 -> 2; matrix products, arithmetic and copies ran while one was open for 8% -> 10% of each run, Pallas kernels for 0% -> 0%
where the time goes in v1:
time: 1300 us; the launch traced here: 1290 us
  waiting for transfers between devices  735 us (57%)
  matrix products  250 us (19%)
  local copies, waits for them, and re-layouts  161 us (12%)
  other arithmetic  91.7 us (7%)
  blocking collectives  26.3 us (2%)
  between operations  16.9 us (1%)
    all_gather x1, waiting for transfers between devices, run_samples_all_by_axis(): work_now = all_gather(m, axis_name='mp')  521 us
    psum x1, waiting for transfers between devices, shards(): normalized_gradient = lax.psum(d_partial, 'mp')  213 us
    dynamic_update_slice x8, local copies, waits for them, and re-layouts, shards(): attn_blocks, log_sums = lax.map(forward_block, starts)  86.6 us
    dot_general x4, matrix products, scores(): jnp.einsum('qhd,khd->hqk', part, key, preferred_element_type=jnp.float32)  36.8 us
    unnamed x46, local copies, waits for them, and re-layouts  29.6 us
    psum x1, blocking collectives, shards(): lax.psum((grad_bias, gain_product, shift_part), 'dp')  26.3 us
  transfers between devices with their start and end apart: 6, of which 2 were waited for; matrix products, arithmetic and copies ran while one was open for 10% of the time, Pallas kernels for 0%

profile of v1, /device:TPU:0, one launch (start us, length us, event | category | flops | bytes accessed | tf_op | source)
XLA Modules:
  0.0 1290.6 jit_solution(4998599029802011729)
XLA Ops:
  8.1 3.0 convert_reduce_fusion
  13.0 8.8 copy.39
  21.9 10.5 broadcast_add_fusion
  45.3 78.8 %while.28 = (s32[]{:T(128)}, f32[2,512,8,64]{1,0,3,2:T(2,128)}, f32[2,8,512]{2,1,0:T(8,128)S(1)}, s32[2]{0:T(128)S(1)}, s32[1024]{0:T(1024)S(1)}, /*index=5*/s32...) while((s32[]{:T(128)}, f32[2,512,8,64]{1,0,3,2:T(2,128)}, ...), condition=%wide.region_8.9_spmd.clone, body=%wide.region_5.8_spmd.clone.sunk | while | flops 1127216640 | bytes 64635112 | solution.py:119
  49.6 4.7 fusion.118
  54.3 4.2 fusion.119
  58.6 4.6 fusion.120
  65.2 19.6 %dynamic_update_slice.19 = f32[2,512,8,64]{1,0,3,2:T(2,128)} dynamic-update-slice(f32[2,512,8,64]{1,0,3,2:T(2,128)} %get-tuple-element.473, f32[1,512,8,64]{1,0,3,2:T(1,128)} %copy.74, s32[]{:T(128)S(6)} %copy.82, s32[]{:T(128)} %constant.40.clone.1..sunk, s32[]{:T(128)} %constant.40.clone.1..sunk, s32[]{:T(128)} %constant.40.clone.1..sunk) | dynamic-update-slice | bytes 2097156 | tf_op jit(solution)/shard_map/while/body/jit(dynamic_update_index_in_dim)/dynamic_update_slice | solution.py:119
  88.9 4.7 fusion.118
  93.6 4.2 fusion.119
  97.9 4.6 fusion.120
  104.5 19.6 %dynamic_update_slice.19 = f32[2,512,8,64]{1,0,3,2:T(2,128)} dynamic-update-slice(f32[2,512,8,64]{1,0,3,2:T(2,128)} %get-tuple-element.473, f32[1,512,8,64]{1,0,3,2:T(1,128)} %copy.74, s32[]{:T(128)S(6)} %copy.82, s32[]{:T(128)} %constant.40.clone.1..sunk, s32[]{:T(128)} %constant.40.clone.1..sunk, s32[]{:T(128)} %constant.40.clone.1..sunk) | dynamic-update-slice | bytes 2097156 | tf_op jit(solution)/shard_map/while/body/jit(dynamic_update_index_in_dim)/dynamic_update_slice | solution.py:119
  124.1 5.5 fusion.62
  131.6 151.9 %while.29 = (s32[]{:T(128)}, f32[1024,8,64]{0,2,1:T(8,128)}, f32[1024,8,64]{0,2,1:T(8,128)}, f32[2,512,8,64]{1,0,3,2:T(2,128)}, s32[2]{0:T(128)S(1)}, /*index=5*...) while((s32[]{:T(128)}, f32[1024,8,64]{0,2,1:T(8,128)}, ...), condition=%wide.region_12.13_spmd.clone, body=%wide.region_10.12_spmd.clone.sunk | while | flops 2732324352 | bytes 171016560 | solution.py:173
  136.0 9.7 fusion.130
  145.7 13.7 %multiply_reduce_fusion.3 = (f32[8,512]{1,0:T(8,128)S(1)}, f32[8,512,1024]{2,1,0:T(8,128)}) fusion(f32[8,512,1024]{2,1,0:T(8,128)} %fusion.130, f32[8,512]{1,0:T(8,128)S(1)} %dynamic-slice_bitcast_fusion.2, bf16[1024,8,64]{0,2,1:T(8,128)(2,1)S(1)} %get-tuple-element.538, bf16[1024,8,64]{0,2,1:T(8,128)(2,1)S(1)} %copy-done.5, s32[]{:T(128)S(6)} %select_n.47, ...), kind=kOutput, calls=%fused_computation.23.clone.1 | convolution fusion | flops 562032640 | bytes 35684356 | tf_op jit(solution)/shard_map/while/body/eval_jaxpr/qhd,khd->hqk/dot_general | solution.py:56
  159.4 11.4 multiply_convert_fusion.8
  170.8 8.8 bitcast_add_fusion.6
  179.6 2.7 fusion.132
  187.5 19.6 %dynamic_update_slice.20 = f32[2,512,8,64]{1,0,3,2:T(2,128)} dynamic-update-slice(f32[2,512,8,64]{1,0,3,2:T(2,128)} %get-tuple-element.517, f32[1,512,8,64]{1,0,3,2:T(1,128)} %copy.75, s32[]{:T(128)S(6)} %copy.92, s32[]{:T(128)} %constant.40.clone.1..sunk.1, s32[]{:T(128)} %constant.40.clone.1..sunk.1, s32[]{:T(128)} %constant.40.clone.1..sunk.1) | dynamic-update-slice | bytes 2097156 | tf_op jit(solution)/shard_map/while/body/jit(dynamic_update_index_in_dim)/dynamic_update_slice | solution.py:119
  211.4 9.7 fusion.130
  221.0 13.7 %multiply_reduce_fusion.3 = (f32[8,512]{1,0:T(8,128)S(1)}, f32[8,512,1024]{2,1,0:T(8,128)}) fusion(f32[8,512,1024]{2,1,0:T(8,128)} %fusion.130, f32[8,512]{1,0:T(8,128)S(1)} %dynamic-slice_bitcast_fusion.2, bf16[1024,8,64]{0,2,1:T(8,128)(2,1)S(1)} %get-tuple-element.538, bf16[1024,8,64]{0,2,1:T(8,128)(2,1)S(1)} %copy-done.5, s32[]{:T(128)S(6)} %select_n.47, ...), kind=kOutput, calls=%fused_computation.23.clone.1 | convolution fusion | flops 562032640 | bytes 35684356 | tf_op jit(solution)/shard_map/while/body/eval_jaxpr/qhd,khd->hqk/dot_general | solution.py:56
  234.8 11.4 multiply_convert_fusion.8
  246.2 9.3 bitcast_add_fusion.6
  255.5 2.7 fusion.132
  263.5 19.6 %dynamic_update_slice.20 = f32[2,512,8,64]{1,0,3,2:T(2,128)} dynamic-update-slice(f32[2,512,8,64]{1,0,3,2:T(2,128)} %get-tuple-element.517, f32[1,512,8,64]{1,0,3,2:T(1,128)} %copy.75, s32[]{:T(128)S(6)} %copy.92, s32[]{:T(128)} %constant.40.clone.1..sunk.1, s32[]{:T(128)} %constant.40.clone.1..sunk.1, s32[]{:T(128)} %constant.40.clone.1..sunk.1) | dynamic-update-slice | bytes 2097156 | tf_op jit(solution)/shard_map/while/body/jit(dynamic_update_index_in_dim)/dynamic_update_slice | solution.py:119
  283.5 4.1 reshape.378
  287.6 2.4 slice.128
  299.9 2.7 convert.64
  305.0 11.2 copy.67
  316.2 15.2 %copy.41 = bf16[2816,2048]{1,0:T(8,128)(2,1)} copy(bf16[2816,2048]{0,1:T(8,128)(2,1)} %bitcast.144) | data formatting | bytes 23068672 | tf_op jit(solution)/shard_map/dot_general | solution.py:121
  331.4 19.1 %fusion.72 = f32[1024,2,1408]{2,0,1:T(8,128)} fusion(bf16[2,1408,2048]{2,1,0:T(8,128)(2,1)} %bitcast.150, bf16[1024,2048]{1,0:T(8,128)(2,1)} %param.15, f32[2048]{0:T(1024)S(1)} %copy-done.23, f32[2048]{0:T(1024)S(1)} %copy-done.19, f32[1024]{0:T(1024)S(1)} %copy-done.17, f32[1024]{0:T(1024)S(1)} %copy-done.15), kind=kOutput, calls=%fused_computation.130 | convolution fusion | flops 11823742976 | bytes 27287552 | tf_op jit(solution)/shard_map/dot_general | solution.py:121
  350.6 16.7 %fusion.59 = (bf16[1024,1,1408]{2,0,1:T(8,128)(2,1)}, bf16[1024,1,1408]{2,0,1:T(8,128)(2,1)}, bf16[1024,1408]{1,0:T(8,128)(2,1)}) fusion(f32[1024,2,1408]{2,0,1:T(8,128)} %fusion.72, bf16[1024,2048]{1,0:T(8,128)(2,1)} %param.25, bf16[1408,2048]{1,0:T(8,128)(2,1)} %param.24), kind=kOutput, calls=%fused_computation.88 | convolution fusion | flops 5927206912 | bytes 30146560 | tf_op jit(solution)/shard_map/to,fo->tf/dot_general | solution.py:143
  367.3 10.1 fusion.69
  377.4 20.1 %bitcast_add_fusion.2 = f32[1024,2048]{1,0:T(8,128)} fusion(f32[1024,2048,1]{1,0,2:T(8,128)} %fusion.69, bf16[2048,2,1408]{2,1,0:T(2,128)(2,1)} %param.23, bf16[1024,1,1408]{2,0,1:T(8,128)(2,1)} %get-tuple-element.289, bf16[1024,1,1408]{2,0,1:T(8,128)(2,1)} %get-tuple-element.288), kind=kOutput, calls=%fused_computation.69 | convolution fusion | flops 11816140800 | bytes 34078720 | tf_op jit(solution)/shard_map/tjf,djf->td/dot_general | solution.py:189
  397.6 20.7 %fusion.57 = f32[2048,2,1408]{2,0,1:T(8,128)} fusion(bf16[1024,1,1408]{2,0,1:T(8,128)(2,1)} %get-tuple-element.289, bf16[1024,1,1408]{2,0,1:T(8,128)(2,1)} %get-tuple-element.288, bf16[1024,2048]{1,0:T(8,128)(2,1)} %param.15, f32[2048]{0:T(1024)S(1)} %copy-done.23, f32[2048]{0:T(1024)S(1)} %copy-done.19, f32[1024]{0:T(1024)S(1)} %copy-done.17, ...), kind=kOutput, calls=%fused_computation.84 | convolution fusion | flops 11835277312 | bytes 33054720 | tf_op jit(solution)/shard_map/td,tjf->djf/dot_general | solution.py:147
  420.5 10.3 fusion.76
  430.8 7.9 convolution_add_fusion
  439.2 9.4 fusion.63
  448.7 12.5 fusion.77
  461.3 14.5 %fusion.68 = f32[2048,3,512]{2,0,1:T(8,128)} fusion(bf16[1024,1,512]{2,0,1:T(8,128)(2,1)} %copy.45, bf16[1024,1,512]{2,0,1:T(8,128)(2,1)} %copy.44, bf16[1024,1,512]{2,0,1:T(8,128)(2,1)S(1)} %copy.43, bf16[1024,2048]{1,0:T(8,128)(2,1)} %param.15, f32[2048]{0:T(1024)S(1)} %copy-done.23, f32[2048]{0:T(1024)S(1)} %copy-done.19, f32[1024]{0:T(1024)S(1)} %copy-done.17, ...), kind=kOutput, calls=%fused_computation.128 | convolution fusion | flops 6464471040 | bytes 19947520 | tf_op jit(solution)/shard_map/td,tjc->djc/dot_general | solution.py:179
  477.8 213.4 %all-reduce.3.cloned.1.call-done = f32[1024,2048]{1,0:T(8,128)} async-done(((f32[1024,2048]{1,0:T(8,128)}), f32[1024,2048]{1,0:T(8,128)}) %all-reduce.3.cloned.1.call-update) | async-done | bytes 8388624 | tf_op jit(solution)/shard_map/psum | solution.py:190
  691.2 7.5 fusion.48
  698.7 26.3 %all-reduce = (f32[2048]{0:T(1024)}, f32[2048]{0:T(1024)}, f32[3,512]{1,0:T(4,128)}) all-reduce(f32[2048]{0:T(1024)S(1)} %get-tuple-element.231, f32[2048]{0:T(1024)S(1)} %get-tuple-element.234, f32[3,512]{1,0:T(4,128)S(1)} %convert_reduce_fusion.1), channel_id=1, replica_groups=mesh['dp'=8,'mp'=4] {'dp'}, use_global_device_ids=true, to_apply=%region_17.18 | all-reduce | flops 5632 | bytes 45056 | tf_op jit(solution)/shard_map/psum | solution.py:200
  725.1 6.7 copy.49
  731.8 521.4 %all-gather.3.cloned.1.call-done = f32[4096,2048]{1,0:T(8,128)} async-done(((f32[1024,2048]{1,0:T(8,128)}), f32[4096,2048]{1,0:T(8,128)}) %all-gather.3.cloned.1.call-update) | async-done | bytes 33554448 | tf_op jit(solution)/shard_map/all_gather | solution.py:78
  1253.2 15.9 %reduce_sum.112 = f32[1024,2048]{1,0:T(8,128)} reduce(f32[4,1024,2048]{2,1,0:T(8,128)} %bitcast.145, f32[]{:T(128)} %constant.41.clone.1), dimensions={0}, to_apply=%region_9.10 | reduce | flops 6291456 | bytes 41943044 | tf_op jit(solution)/shard_map/reduce_sum | solution.py:79
  1269.1 13.7 %fusion.47 = (bf16[1024,2048]{1,0:T(8,128)(2,1)}, bf16[1024,2048]{1,0:T(8,128)(2,1)}) fusion(bf16[1024,2048]{1,0:T(8,128)(2,1)} %param.15, bf16[1024,2048]{1,0:T(8,128)(2,1)} %param.25, f32[1024,2048]{1,0:T(8,128)} %all-reduce.3.cloned.1.call-done, f32[1024]{0:T(1024)S(1)} %broadcast_multiply_fusion, f32[1024]{0:T(1024)S(1)} %broadcast_multiply_fusion.1, ...), kind=kLoop, calls=%fused_computation.65 | loop fusion | flops 27262976 | bytes 33579008 | tf_op jit(solution)/shard_map/convert_element_type | solution.py:199
  (144 shorter events, 56.6 us)
Async XLA Ops:
  8.0 116.1 %copy-start = (bf16[512,2048]{1,0:T(8,128)(2,1)S(1)}, bf16[512,2048]{1,0:T(8,128)(2,1)}, u32[]{:S(2)}) copy-start(bf16[512,2048]{1,0:T(8,128)(2,1)} %param.22) | copy-start | bytes 6291460
  8.0 683.2 %all-reduce.3.cloned.1.call-start = ((), (), s32[]{:S(2)}) async-start(), calls=%async_computation.4 | async-start | bytes 16777216 | tf_op jit(solution)/shard_map/psum | solution.py:190
  8.1 3.6 copy-start.4
  11.7 10.1 copy-start.14
  12.9 8.9 copy-start.16
  13.0 8.9 copy-start.18
  13.0 8.9 copy-start.21
  13.0 8.9 copy-start.22
  32.4 4.1 copy-start.9
  40.8 1.4 copy-start.10
  40.8 1.4 copy-start.12
  45.3 78.8 %copy-start.20 = (bf16[1024]{0:T(1024)(128)(2,1)S(1)}, bf16[1024]{0:T(1024)(128)(2,1)}, u32[]{:S(2)}) copy-start(bf16[1024]{0:T(1024)(128)(2,1)} %fusion.65) | copy-start | bytes 6148
  54.3 4.3 copy-start.3
  93.6 4.3 copy-start.3
  136.0 9.7 copy-start.5
  159.4 11.4 copy-start.6
  179.6 2.7 copy-start.1
  184.2 1.3 copy-start.2
  211.3 9.7 copy-start.5
  234.8 11.4 copy-start.6
  255.5 2.7 copy-start.1
  260.1 1.3 copy-start.2
  283.5 6.5 copy-start.11
  283.5 6.5 copy-start.13
  316.2 15.2 %copy-start.15 = (f32[1024]{0:T(1024)S(1)}, f32[1024]{0:T(1024)}, u32[]{:S(2)}) copy-start(f32[1024]{0:T(1024)} %copy-done.14) | copy-start | bytes 12292
  316.2 15.2 %copy-start.17 = (f32[1024]{0:T(1024)S(1)}, f32[1024]{0:T(1024)}, u32[]{:S(2)}) copy-start(f32[1024]{0:T(1024)} %copy-done.16) | copy-start | bytes 12292
  316.2 15.2 %copy-start.19 = (f32[2048]{0:T(1024)S(1)}, f32[2048]{0:T(1024)}, u32[]{:S(2)}) copy-start(f32[2048]{0:T(1024)} %param.18) | copy-start | bytes 24580
  316.2 15.2 %copy-start.23 = (f32[2048]{0:T(1024)S(1)}, f32[2048]{0:T(1024)}, u32[]{:S(2)}) copy-start(f32[2048]{0:T(1024)} %param.19) | copy-start | bytes 24580
  331.4 35.8 %slice-start = ((s8[6291456]{0:T(1024)(128)(4,1)}), s8[4194304]{0:T(1024)(128)(4,1)S(1)}, s32[]{:S(2)}) async-start(s8[6291456]{0:T(1024)(128)(4,1)} %bitcast.152), calls=%async_computation.10 | async-start | bytes 8388608
  350.6 16.7 %slice-start.1 = ((s8[6291456]{0:T(1024)(128)(4,1)}), s8[2097152]{0:T(1024)(128)(4,1)S(1)}, s32[]{:S(2)}) async-start(s8[6291456]{0:T(1024)(128)(4,1)} %bitcast.152), calls=%async_computation.11 | async-start | bytes 4194304
  350.6 16.7 %copy-start.8 = (bf16[1024,1,512]{2,0,1:T(8,128)(2,1)S(1)}, bf16[1024,1,512]{2,0,1:T(8,128)(2,1)}, u32[]{:S(2)}) copy-start(bf16[1024,1,512]{2,0,1:T(8,128)(2,1)} %copy.44) | copy-start | bytes 3145732
  397.5 327.5 %reduce-scatter.9.cloned.1.call-start = ((), (), s32[]{:S(2)}) async-start(), calls=%async_computation.7 | async-start | bytes 25952256 | tf_op jit(solution)/shard_map/reduce_scatter | solution.py:184
  418.3 834.9 %all-gather.3.cloned.1.call-start = ((), (), s32[]{:S(2)}) async-start(), calls=%async_computation.9 | async-start | bytes 41943040 | tf_op jit(solution)/shard_map/all_gather | solution.py:78
  420.4 10.4 copy-start.7
  438.8 844.0 %reduce-scatter.7.cloned.1.call-start = ((), (), s32[]{:S(2)}) async-start(), calls=%async_computation.6 | async-start | bytes 4718592 | tf_op jit(solution)/shard_map/reduce_scatter | solution.py:183
  448.7 834.1 %reduce-scatter.11.cloned.1.call-start = ((), (), s32[]{:S(2)}) async-start(), calls=%async_computation.8 | async-start | bytes 12976128 | tf_op jit(solution)/shard_map/reduce_scatter | solution.py:185
  461.2 821.6 %reduce-scatter.5.cloned.1.call-start = ((), (), s32[]{:S(2)}) async-start(), calls=%async_computation.5 | async-start | bytes 14155776 | tf_op jit(solution)/shard_map/reduce_scatter | solution.py:182
Sparse Core Ops, SparseCore 0:
  397.7 293.5 all-reduce.2
  692.8 560.3 all-gather.2
Sparse Core Ops, SparseCore 1:
  418.4 148.9 reduce-scatter.8
  571.1 50.9 reduce-scatter.6
  626.0 86.9 reduce-scatter.10
  717.1 92.0 reduce-scatter.4
